TPU v7x, 32 devices: a whole 2x2x4 slice. The times are simulated.
32 devices in a mesh: gx: 4 (over y, x), gy: 8 (over z, core).
Axes of the slice: x: 2, y: 2, z: 4, core: 2. Of those that a mesh axis runs over, the one named last changes fastest.
Arguments:
- old_state: float32 [8, 8, 128, 1024], P(None, None, 'gx', 'gy'), may hold values from -6 to 6
- section_prims: float32 [8, 8, 128, 1024], P(None, None, 'gx', 'gy'), may hold values from -3 to 3, as said below
- shear_whole: int32 [1], replicated, may hold values from 0 to 1023
- shear_frac: float32 [1], replicated, may hold values from 0 to 1
Outputs:
- new_state: float32 [8, 8, 128, 1024], P(None, None, 'gx', 'gy')
Inputs may be any that keep to these rules, and one draw needn't show every extreme that they name: section_prims holds density in [0.5, 2] in field 0 and pressure in [0.3, 3] in field 4; the other fields lie in the stated range.
All inputs are finite; a program needn't handle non-finite values.
Results may differ from a plain program's by a relative error of at most 0.0003.
Values sent between devices are 32-bit elements; how exact they have to be, the bound alone decides.
No kernel may reach another device: no remote copies, remote signals or barrier semaphores. Data moves between devices by JAX's collectives and lax.ppermute only.
A program may use at most 128 MiB of HBM per device.

v0:
```python
import jax
import jax.numpy as jnp
from jax import lax
from jax.sharding import PartitionSpec as P

gamma_gas = 5.0 / 3.0
omega_rate = 1.0
shear_rate = 1.5
time_step = 0.1


def with_halo(shard, sides, width):
    for axis, dim in sides:
        size, length = (lax.axis_size(axis), shard.shape[dim])
        up = [(i, (i + 1) % size) for i in range(size)]
        down = [(j, i) for i, j in up]
        last = lax.slice_in_dim(shard, length - width, length, axis=dim)
        first = lax.slice_in_dim(shard, 0, width, axis=dim)
        before = lax.ppermute(last, axis, up)
        after = lax.ppermute(first, axis, down)
        shard = jnp.concatenate([before, shard, after], axis=dim)
    return shard


def conserved(prims):
    rho = prims[0]
    kinetic = 0.5 * rho * (prims[1] * prims[1] + prims[2] * prims[2] + prims[3] * prims[3])
    magnetic = 0.5 * (prims[5] * prims[5] + prims[6] * prims[6] + prims[7] * prims[7])
    energy = prims[4] / (gamma_gas - 1.0) + kinetic + magnetic
    return jnp.stack(
        [rho, rho * prims[1], rho * prims[2], rho * prims[3], energy, prims[5], prims[6], prims[7]]
    )


def fluxes(prims, cons, direction):
    rho = prims[0]
    normal_vel = prims[1 + direction]
    normal_mag = prims[5 + direction]
    ptotal = prims[4] + 0.5 * (prims[5] * prims[5] + prims[6] * prims[6] + prims[7] * prims[7])
    vdotb = prims[1] * prims[5] + prims[2] * prims[6] + prims[3] * prims[7]
    parts = [rho * normal_vel]
    for comp in range(3):
        parts.append(rho * prims[1 + comp] * normal_vel - prims[5 + comp] * normal_mag)
    parts[1 + direction] = parts[1 + direction] + ptotal
    parts.append((cons[4] + ptotal) * normal_vel - normal_mag * vdotb)
    for comp in range(3):
        parts.append(prims[5 + comp] * normal_vel - prims[1 + comp] * normal_mag)
    return jnp.stack(parts)


def fast_speed(prims, direction):
    rho = prims[0]
    sound = gamma_gas * prims[4] / rho
    squares = [prims[5] * prims[5], prims[6] * prims[6], prims[7] * prims[7]]
    alfven = (squares[0] + squares[1] + squares[2]) / rho
    others = [squares[c] for c in range(3) if c != direction]
    transverse = (others[0] + others[1]) / rho
    disc = jnp.square(sound - alfven) + 4.0 * sound * transverse
    return jnp.sqrt(0.5 * (sound + alfven + jnp.sqrt(disc)))


def minmod(first, second):
    return 0.5 * (jnp.sign(first) + jnp.sign(second)) * jnp.minimum(jnp.abs(first), jnp.abs(second))


def rusanov(left, right, direction):
    cons_left = conserved(left)
    cons_right = conserved(right)
    flux_left = fluxes(left, cons_left, direction)
    flux_right = fluxes(right, cons_right, direction)
    speed_left = jnp.abs(left[1 + direction]) + fast_speed(left, direction)
    speed_right = jnp.abs(right[1 + direction]) + fast_speed(right, direction)
    speed = jnp.maximum(speed_left, speed_right)
    return 0.5 * (flux_left + flux_right) - 0.5 * speed * (cons_right - cons_left)


def sweep(padded, axis, direction):
    length = padded.shape[axis]
    cells = length - 4

    def take(arr, start, stop):
        return lax.slice_in_dim(arr, start, stop, axis=axis)

    diff = take(padded, 1, length) - take(padded, 0, length - 1)
    slope = minmod(take(diff, 0, length - 2), take(diff, 1, length - 1))
    left = take(padded, 1, length - 2) + 0.5 * take(slope, 0, length - 3)
    right = take(padded, 2, length - 1) - 0.5 * take(slope, 1, length - 2)
    face = rusanov(left, right, direction)
    return take(face, 1, cells + 1) - take(face, 0, cells)


def sources(core):
    rho = core[0]
    zeros = jnp.zeros_like(rho)
    return jnp.stack(
        [
            zeros,
            2.0 * omega_rate * rho * core[2],
            -(2.0 - shear_rate) * omega_rate * rho * core[1],
            zeros,
            shear_rate * omega_rate * (rho * core[1] * core[2] - core[5] * core[6]),
            zeros,
            -shear_rate * omega_rate * core[5],
            zeros,
        ]
    )


def section_update(radial_rows, azimuthal_rows, old):
    core = azimuthal_rows[:, :, :, 2:-2]
    radial = sweep(radial_rows, 2, 0)
    azimuthal = sweep(azimuthal_rows, 3, 1)
    zpadded = jnp.concatenate([core[:, -2:], core, core[:, :2]], axis=1)
    vertical = sweep(zpadded, 1, 2)
    rates = -(radial + azimuthal + vertical) + sources(core)
    return 0.5 * old + 0.5 * (conserved(core) + time_step * rates)


def on_device(old_state, section_prims, shear_whole, shear_frac):
    padded = with_halo(section_prims, (("gx", 2), ("gy", 3)), 2)
    cells = section_prims.shape[3]
    loop_size = lax.axis_size("gy")
    total = cells * loop_size
    shift_cells = shear_whole[0]
    frac = shear_frac[0]
    back_cells = (total - 1 - shift_cells) % total
    inner_src = padded[:, :, 0:2, 2:-2]
    outer_src = padded[:, :, -2:, 2:-2]
    inner_cycle, outer_cycle = (
        lax.all_gather(inner_src, "gy", axis=3, tiled=True),
        lax.all_gather(outer_src, "gy", axis=3, tiled=True),
    )
    position = lax.axis_index("gy") * cells
    inner_ext = jnp.concatenate([inner_cycle, inner_cycle[..., : cells + 1]], axis=3)
    outer_ext = jnp.concatenate([outer_cycle, outer_cycle[..., : cells + 1]], axis=3)
    inner_win = lax.dynamic_slice_in_dim(inner_ext, (position + shift_cells) % total, cells + 1, 3)
    outer_win = lax.dynamic_slice_in_dim(outer_ext, (position + back_cells) % total, cells + 1, 3)
    inner_ghost = (1.0 - frac) * inner_win[..., :cells] + frac * inner_win[..., 1:]
    outer_ghost = (1.0 - frac) * outer_win[..., 1:] + frac * outer_win[..., :cells]
    radial_index = lax.axis_index("gx")
    left_rows = jnp.where(radial_index == 0, inner_ghost, inner_src)
    right_rows = jnp.where(radial_index == lax.axis_size("gx") - 1, outer_ghost, outer_src)
    azimuthal_rows = padded[:, :, 2:-2, :]
    radial_rows = jnp.concatenate([left_rows, azimuthal_rows[:, :, :, 2:-2], right_rows], axis=2)
    return section_update(radial_rows, azimuthal_rows, old_state)


def solution(mesh):
    in_specs = (P(None, None, "gx", "gy"), P(None, None, "gx", "gy"), P(), P())
    out_specs = P(None, None, "gx", "gy")
    return jax.shard_map(
        on_device, mesh=mesh, in_specs=in_specs, out_specs=out_specs, check_vma=False
    )
```

profile of v0, /device:TPU:0, one launch (start us, length us, event | category | flops | bytes accessed | tf_op | source)
XLA Modules:
  0.0 111.1 jit_solution(10720879476394507808)
XLA Ops:
  0.0 1.9 %copy.188 = f32[8,8,32,128]{3,1,2,0:T(8,128)S(1)} copy(f32[8,8,32,128]{3,2,1,0:T(8,128)} %param.5) | data formatting | bytes 2097152 | tf_op args[1]
  1.9 1.0 copy-done.4
  3.6 3.9 %collective-permute-start.1 = (f32[8,8,2,128]{3,1,2,0:T(8,128)}, f32[8,8,2,128]{3,1,2,0:T(8,128)S(1)}, u32[]{:S(2)}, u32[]{:S(2)}) collective-permute-start(f32[8,8,2,128]{3,1,2,0:T(8,128)} %get-tuple-element.78), channel_id=1, source_target_pairs={{8,0},{16,8},{24,16},{0,24},{9,1},{17,9},{25,17},{1,25},{10,2},{18... | collective-permute-start | bytes 196616 | tf_op jit(solution)/shard_map/ppermute | solution.py:20
  8.4 1.7 %pad_maximum_fusion.5 = (f32[8,9,32,128]{3,2,1,0:T(8,128)}, f32[8,9,32,128]{3,2,1,0:T(8,128)}) fusion(f32[8,8,32,128]{3,2,1,0:T(8,128)S(1)} %copy-done.1, f32[8,2,32,128]{3,2,1,0:T(8,128)S(1)} %get-tuple-element.82, f32[8,2,32,128]{3,2,1,0:T(8,128)S(1)} %get-tuple-element.83), kind=kLoop, calls=%fused_computation.19 | loop fusion | flops 589824 | bytes 3932160 | tf_op jit(solution)/shard_map/concatenate | solution.py:113
  12.4 2.1 %copy_subtract_fusion = f32[8,11,32,128]{3,1,2,0:T(8,128)S(1)} fusion(f32[8,11,32,128]{3,2,1,0:T(8,128)S(1)} %get-tuple-element.51, f32[8,11,32,128]{3,2,1,0:T(8,128)S(1)} %get-tuple-element.50), kind=kLoop, calls=%fused_computation.12 | loop fusion | flops 360448 | bytes 4325376 | tf_op jit(solution)/shard_map/sub | solution.py:84
  14.5 1.5 %minimum_multiply_fusion = f32[8,10,32,128]{3,1,2,0:T(8,128)S(1)} fusion(f32[8,11,32,128]{3,1,2,0:T(8,128)S(1)} %copy_subtract_fusion), kind=kLoop, calls=%fused_computation.14 | loop fusion | flops 2621440 | bytes 3932160 | tf_op jit(solution)/shard_map/mul | solution.py:63
  16.1 2.2 %fusion.1 = (f32[8,9,32,128]{3,1,2,0:T(8,128)S(1)}, f32[8,9,32,128]{3,1,2,0:T(8,128)S(1)}) fusion(f32[8,10,32,128]{3,1,2,0:T(8,128)S(1)} %minimum_multiply_fusion, f32[8,9,32,128]{3,2,1,0:T(8,128)S(1)} %copy-done.8, f32[8,9,32,128]{3,2,1,0:T(8,128)S(1)} %copy-done.9), kind=kLoop, calls=%fused_computation.4 | loop fusion | flops 1179648 | bytes 7077888 | tf_op jit(solution)/shard_map/add | solution.py:86
  18.5 1.3 %multiply_bitcast_fusion = (f32[9,32,128]{2,0,1:T(8,128)}, f32[1,9,32,128]{3,1,2,0:T(8,128)S(1)}, f32[1,9,32,128]{3,1,2,0:T(8,128)S(1)}, f32[8,9,32,128]{3,1,2,0:T(8,128)S(1)}) fusion(f32[8,9,32,128]{3,1,2,0:T(8,128)S(1)} %get-tuple-element.49, f32[8,9,32,128]{3,1,2,0:T(8,128)S(1)} %get-tuple-element.48, ...), kind=kLoop, calls=%fused_computation.52 | loop fusion | flops 1622016 | bytes 4341760 | tf_op jit(solution)/shard_map/mul | solution.py:74
  23.6 0.9 subtract_dynamic-update-slice_fusion.9
  31.2 0.8 constant_dynamic-update-slice_fusion.59
  32.0 0.8 slice_dynamic-update-slice_fusion.6
  33.6 2.1 %constant_dynamic-update-slice_fusion.53 = f32[8,9,32,128]{3,1,2,0:T(8,128)} fusion(f32[8,9,32,128]{3,1,2,0:T(8,128)} %constant_dynamic-update-slice_fusion.54, f32[1,9,32,128]{3,1,2,0:T(8,128)} %get-tuple-element.25), kind=kLoop, calls=%fused_computation.157 | loop fusion | bytes 524288
  35.7 2.5 %slice_dynamic-update-slice_fusion = (f32[8,9,32,128]{3,1,2,0:T(8,128)}, f32[8,9,32,128]{3,1,2,0:T(8,128)}) fusion(f32[8,9,32,128]{3,1,2,0:T(8,128)} %constant_dynamic-update-slice_fusion.53, f32[8,9,32,128]{3,1,2,0:T(8,128)} %copy-done, f32[8,9,32,128]{3,1,2,0:T(8,128)} %constant_dynamic-update-slice_fusion.48, f32[8,9,32,128]{3,1,2,0:T(8,128)S(1)} %get-tuple-element.49), kind=kLoop, calls=%fused_computation.41 | loop fusion | bytes 2801664 | tf_op jit(solution)/shard_map/stack | solution.py:30
  38.2 4.1 %multiply_subtract_fusion = f32[8,9,32,128]{3,1,2,0:T(8,128)} fusion(f32[8,9,32,128]{3,1,2,0:T(8,128)} %get-tuple-element.89, f32[8,9,32,128]{3,1,2,0:T(8,128)} %get-tuple-element.88, f32[8,9,32,128]{3,1,2,0:T(8,128)S(1)} %copy-done.13, f32[8,9,32,128]{3,1,2,0:T(8,128)S(1)} %copy-done.11, f32[9,32,128]{2,0,1:T(8,128)} %get-tuple-element.19), kind=kLoop, calls=%fused_computation.13 | loop fusion | flops 1474560 | bytes 6045696 | tf_op jit(solution)/shard_map/sub | solution.py:74
  43.0 15.0 %all_gather.7 = f32[8,8,2,1024]{3,1,2,0:T(8,128)S(1)} all-gather(f32[8,8,2,128]{3,1,2,0:T(8,128)S(1)} %collective-permute-done.1), channel_id=1, replica_groups=mesh['gx'=4,'gy'=8] {'gy'}, dimensions={3}, use_global_device_ids=true | all-gather | bytes 589824 | tf_op jit(solution)/shard_map/all_gather | solution.py:131
  58.1 15.1 %all_gather.6 = f32[8,8,2,1024]{3,1,2,0:T(8,128)S(1)} all-gather(f32[8,8,2,128]{3,1,2,0:T(8,128)S(1)} %collective-permute-done), channel_id=1, replica_groups=mesh['gx'=4,'gy'=8] {'gy'}, dimensions={3}, use_global_device_ids=true | all-gather | bytes 589824 | tf_op jit(solution)/shard_map/all_gather | solution.py:130
  75.2 0.9 multiply_bitcast_fusion.2
  77.1 1.0 constant_dynamic-update-slice_fusion.8
  78.1 1.0 copy-done.16
  79.1 1.4 %fusion.21 = (f32[8,8,36,2]{3,1,2,0:T(8,128)}, f32[8,8,36,2]{3,1,2,0:T(8,128)S(1)}) fusion(f32[8,8,36,128]{3,1,2,0:T(8,128)S(1)} %get-tuple-element.87), kind=kLoop, calls=%fused_computation.205 | loop fusion | bytes 73728 | tf_op jit(solution)/shard_map/slice | solution.py:17
  80.5 1.8 %copy.194 = f32[8,8,36,2]{2,1,3,0:T(8,128)S(1)} copy(f32[8,8,36,2]{3,1,2,0:T(8,128)} %get-tuple-element.52) | data formatting | bytes 36864 | tf_op jit(solution)/shard_map/slice | solution.py:17
  82.7 1.2 %copy.196 = f32[8,8,36,2]{2,1,3,0:T(8,128)} copy(f32[8,8,36,2]{3,1,2,0:T(8,128)S(1)} %get-tuple-element.53) | data formatting | bytes 36864 | tf_op jit(solution)/shard_map/slice | solution.py:18
  83.9 3.4 %collective-permute-start.3 = (f32[8,8,36,2]{2,1,3,0:T(8,128)}, f32[8,8,36,2]{2,1,3,0:T(8,128)}, u32[]{:S(2)}, u32[]{:S(2)}) collective-permute-start(f32[8,8,36,2]{2,1,3,0:T(8,128)} %copy.196), channel_id=1, source_target_pairs={{1,0},{2,1},{3,2},{4,3},{5,4},{6,5},{7,6},{0,7},{9,8},{10,9},{11,1... | collective-permute-start | bytes 55304 | tf_op jit(solution)/shard_map/ppermute | solution.py:20
  90.4 1.1 copy-done.15
  91.8 1.2 %multiply_subtract_fusion.2 = f32[8,8,33,128]{3,1,2,0:T(8,128)} fusion(f32[8,8,33,128]{3,1,2,0:T(8,128)S(1)} %get-tuple-element.93, f32[8,8,33,128]{3,1,2,0:T(8,128)S(1)} %get-tuple-element.92, f32[8,8,33,128]{3,1,2,0:T(8,128)S(1)} %get-tuple-element.60, f32[8,8,33,128]{3,1,2,0:T(8,128)S(1)} %copy-done.19, f32[8,33,128]{2,0,1:T(8,128)S(1)} %get-tuple-element.5), kind=kLoop, calls=%fused_computation.29 | loop fusion | flops 1351680 | bytes 5541888 | tf_op jit(solution)/shard_map/sub | solution.py:74
  92.9 1.5 %copy.195 = f32[8,8,36,2]{3,1,2,0:T(8,128)S(1)} copy(f32[8,8,36,2]{2,1,3,0:T(8,128)} %collective-permute-done.2) | data formatting | bytes 36864 | tf_op jit(solution)/shard_map/ppermute | solution.py:19
  94.5 1.4 %copy.198 = f32[8,8,36,2]{3,1,2,0:T(8,128)S(1)} copy(f32[8,8,36,2]{2,1,3,0:T(8,128)} %collective-permute-done.3) | data formatting | bytes 36864 | tf_op jit(solution)/shard_map/ppermute | solution.py:20
  95.9 1.0 pad_maximum_fusion
  97.5 1.4 %minimum_multiply_fusion.1 = f32[8,8,32,130]{3,1,2,0:T(8,128)S(1)} fusion(f32[8,8,32,131]{3,1,2,0:T(8,128)S(1)} %slice_subtract_fusion), kind=kLoop, calls=%fused_computation.16 | loop fusion | flops 2129920 | bytes 3194880 | tf_op jit(solution)/shard_map/mul | solution.py:63
  99.0 1.5 %fusion.3 = (f32[8,8,32,129]{3,1,2,0:T(8,128)S(1)}, f32[8,8,32,129]{3,1,2,0:T(8,128)S(1)}) fusion(f32[8,8,32,130]{3,1,2,0:T(8,128)S(1)} %minimum_multiply_fusion.1, f32[8,8,36,128]{3,1,2,0:T(8,128)S(1)} %copy-done.3, f32[8,8,36,2]{3,1,2,0:T(8,128)S(1)} %copy.195, f32[8,8,36,2]{3,1,2,0:T(8,128)S(1)} %copy.198), kind=kLoop, calls=%fused_computation.9 | loop fusion | flops 1585152 | bytes 5443584 | tf_op jit(solution)/shard_map/add | solution.py:86
  105.1 4.8 %fusion.12 = f32[8,8,32,128]{3,1,2,0:T(8,128)S(1)} fusion(f32[8,9,32,128]{3,1,2,0:T(8,128)S(1)} %copy-done.7, f32[8,8,32,129]{3,1,2,0:T(8,128)S(1)} %multiply_subtract_fusion.1, f32[8,8,33,128]{3,1,2,0:T(8,128)S(1)} %copy-done.6, f32[8,8,32,128]{3,2,1,0:T(8,128)S(1)} %copy-done.20, f32[8,8,32,128]{3,2,1,0:T(8,128)} %slice_dynamic-update-slice_fusion.6, ...), kind=kLoop, calls=%fused_computation.37 | loop fusion | flops 2883584 | bytes 10485760 | tf_op jit(solution)/shard_map/add | solution.py:116
  109.9 1.2 %copy.207 = f32[8,8,32,128]{3,2,1,0:T(8,128)} copy(f32[8,8,32,128]{3,1,2,0:T(8,128)S(1)} %fusion.12) | data formatting | bytes 2097152 | tf_op jit(solution)/shard_map/add | solution.py:116
  (132 shorter events, 26.4 us)
Async XLA Ops:
  0.0 8.2 %copy-start.1 = (f32[8,8,32,128]{3,2,1,0:T(8,128)S(1)}, f32[8,8,32,128]{3,2,1,0:T(8,128)}, u32[]{:S(2)}) copy-start(f32[8,8,32,128]{3,2,1,0:T(8,128)} %param.5) | copy-start | bytes 3145732
  1.9 1.0 copy-start.4
  3.6 39.4 %collective-permute-start.1 = (f32[8,8,2,128]{3,1,2,0:T(8,128)}, f32[8,8,2,128]{3,1,2,0:T(8,128)S(1)}, u32[]{:S(2)}, u32[]{:S(2)}) collective-permute-start(f32[8,8,2,128]{3,1,2,0:T(8,128)} %get-tuple-element.78), channel_id=1, source_target_pairs={{8,0},{16,8},{24,16},{0,24},{9,1},{17,9},{25,17},{1,25},{10,2},{18... | collective-permute-start | bytes 196616 | tf_op jit(solution)/shard_map/ppermute | solution.py:20
  7.5 50.6 %collective-permute-start = (f32[8,8,2,128]{3,1,2,0:T(8,128)}, f32[8,8,2,128]{3,1,2,0:T(8,128)S(1)}, u32[]{:S(2)}, u32[]{:S(2)}) collective-permute-start(f32[8,8,2,128]{3,1,2,0:T(8,128)} %get-tuple-element.79), channel_id=1, source_target_pairs={{0,8},{8,16},{16,24},{24,0},{1,9},{9,17},{17,25},{25,1},{2,10},{10... | collective-permute-start | bytes 196616 | tf_op jit(solution)/shard_map/ppermute | solution.py:19
  14.5 1.5 %copy-start.8 = (f32[8,9,32,128]{3,2,1,0:T(8,128)S(1)}, f32[8,9,32,128]{3,2,1,0:T(8,128)}, u32[]{:S(2)}) copy-start(f32[8,9,32,128]{3,2,1,0:T(8,128)} %get-tuple-element.80) | copy-start | bytes 3538948
  14.5 1.6 %copy-start.9 = (f32[8,9,32,128]{3,2,1,0:T(8,128)S(1)}, f32[8,9,32,128]{3,2,1,0:T(8,128)}, u32[]{:S(2)}) copy-start(f32[8,9,32,128]{3,2,1,0:T(8,128)} %get-tuple-element.81) | copy-start | bytes 3538948
  18.3 8.5 %copy-start = (f32[8,9,32,128]{3,1,2,0:T(8,128)}, f32[8,9,32,128]{3,1,2,0:T(8,128)S(1)}, u32[]{:S(2)}) copy-start(f32[8,9,32,128]{3,1,2,0:T(8,128)S(1)} %get-tuple-element.48) | copy-start | bytes 3538948
  21.3 3.2 %copy-start.10 = (f32[8,9,32,128]{3,1,2,0:T(8,128)}, f32[8,9,32,128]{3,1,2,0:T(8,128)S(1)}, u32[]{:S(2)}) copy-start(f32[8,9,32,128]{3,1,2,0:T(8,128)S(1)} %get-tuple-element.43) | copy-start | bytes 3538948
  25.4 5.2 %copy-start.12 = (f32[8,9,32,128]{3,1,2,0:T(8,128)}, f32[8,9,32,128]{3,1,2,0:T(8,128)S(1)}, u32[]{:S(2)}) copy-start(f32[8,9,32,128]{3,1,2,0:T(8,128)S(1)} %get-tuple-element.45) | copy-start | bytes 3538948
  32.9 5.4 %copy-start.11 = (f32[8,9,32,128]{3,1,2,0:T(8,128)S(1)}, f32[8,9,32,128]{3,1,2,0:T(8,128)}, u32[]{:S(2)}) copy-start(f32[8,9,32,128]{3,1,2,0:T(8,128)} %copy-done.10) | copy-start | bytes 3538948
  32.9 5.4 %copy-start.13 = (f32[8,9,32,128]{3,1,2,0:T(8,128)S(1)}, f32[8,9,32,128]{3,1,2,0:T(8,128)}, u32[]{:S(2)}) copy-start(f32[8,9,32,128]{3,1,2,0:T(8,128)} %copy-done.12) | copy-start | bytes 3538948
  73.2 1.2 %copy-start.5 = (f32[8,8,32,128]{3,1,2,0:T(8,128)S(1)}, f32[8,8,32,128]{3,1,2,0:T(8,128)}, u32[]{:S(2)}) copy-start(f32[8,8,32,128]{3,1,2,0:T(8,128)} %copy-done.4) | copy-start | bytes 3145732
  74.3 4.8 %copy-start.2 = (f32[8,8,36,128]{3,1,2,0:T(8,128)}, f32[8,8,36,128]{3,1,2,0:T(8,128)S(1)}, u32[]{:S(2)}) copy-start(f32[8,8,36,128]{3,1,2,0:T(8,128)S(1)} %get-tuple-element.87) | copy-start | bytes 3538948
  76.9 1.2 %copy-start.18 = (f32[8,8,33,128]{3,1,2,0:T(8,128)}, f32[8,8,33,128]{3,1,2,0:T(8,128)S(1)}, u32[]{:S(2)}) copy-start(f32[8,8,33,128]{3,1,2,0:T(8,128)S(1)} %get-tuple-element.8) | copy-start | bytes 3244036
  78.1 1.0 copy-start.16
  82.3 10.7 %collective-permute-start.2 = (f32[8,8,36,2]{2,1,3,0:T(8,128)S(1)}, f32[8,8,36,2]{2,1,3,0:T(8,128)}, u32[]{:S(2)}, u32[]{:S(2)}) collective-permute-start(f32[8,8,36,2]{2,1,3,0:T(8,128)S(1)} %copy.194), channel_id=1, source_target_pairs={{0,1},{1,2},{2,3},{3,4},{4,5},{5,6},{6,7},{7,0},{8,9},{9,10},{10,1... | collective-permute-start | bytes 55304 | tf_op jit(solution)/shard_map/ppermute | solution.py:19
  83.9 5.6 %copy-start.22 = (f32[1,8,33,128]{3,1,2,0:T(8,128)S(1)}, f32[1,8,33,128]{3,1,2,0:T(8,128)}, u32[]{:S(2)}) copy-start(f32[1,8,33,128]{3,1,2,0:T(8,128)} %get-tuple-element.9) | copy-start | bytes 405508
  83.9 6.3 %copy-start.14 = (f32[8,8,33,128]{3,1,2,0:T(8,128)S(1)}, f32[8,8,33,128]{3,1,2,0:T(8,128)}, u32[]{:S(2)}) copy-start(f32[8,8,33,128]{3,1,2,0:T(8,128)} %get-tuple-element.66) | copy-start | bytes 3244036
  83.9 6.3 %copy-start.17 = (f32[8,8,33,128]{3,1,2,0:T(8,128)S(1)}, f32[8,8,33,128]{3,1,2,0:T(8,128)}, u32[]{:S(2)}) copy-start(f32[8,8,33,128]{3,1,2,0:T(8,128)} %copy-done.16) | copy-start | bytes 3244036
  83.9 10.6 %collective-permute-start.3 = (f32[8,8,36,2]{2,1,3,0:T(8,128)}, f32[8,8,36,2]{2,1,3,0:T(8,128)}, u32[]{:S(2)}, u32[]{:S(2)}) collective-permute-start(f32[8,8,36,2]{2,1,3,0:T(8,128)} %copy.196), channel_id=1, source_target_pairs={{1,0},{2,1},{3,2},{4,3},{5,4},{6,5},{7,6},{0,7},{9,8},{10,9},{11,1... | collective-permute-start | bytes 55304 | tf_op jit(solution)/shard_map/ppermute | solution.py:20
  88.8 1.6 %copy-start.21 = (f32[1,8,33,128]{3,1,2,0:T(8,128)S(1)}, f32[1,8,33,128]{3,1,2,0:T(8,128)}, u32[]{:S(2)}) copy-start(f32[1,8,33,128]{3,1,2,0:T(8,128)} %get-tuple-element.11) | copy-start | bytes 405508
  90.2 1.2 %copy-start.15 = (f32[8,8,33,128]{3,1,2,0:T(8,128)S(1)}, f32[8,8,33,128]{3,1,2,0:T(8,128)}, u32[]{:S(2)}) copy-start(f32[8,8,33,128]{3,1,2,0:T(8,128)} %constant_dynamic-update-slice_fusion.21) | copy-start | bytes 3244036
  90.2 1.6 %copy-start.19 = (f32[8,8,33,128]{3,1,2,0:T(8,128)S(1)}, f32[8,8,33,128]{3,1,2,0:T(8,128)}, u32[]{:S(2)}) copy-start(f32[8,8,33,128]{3,1,2,0:T(8,128)} %get-tuple-element.54) | copy-start | bytes 3244036
  92.9 2.9 %copy-start.3 = (f32[8,8,36,128]{3,1,2,0:T(8,128)S(1)}, f32[8,8,36,128]{3,1,2,0:T(8,128)}, u32[]{:S(2)}) copy-start(f32[8,8,36,128]{3,1,2,0:T(8,128)} %copy-done.2) | copy-start | bytes 3538948
  102.9 1.2 %copy-start.6 = (f32[8,8,33,128]{3,1,2,0:T(8,128)S(1)}, f32[8,8,33,128]{3,1,2,0:T(8,128)}, u32[]{:S(2)}) copy-start(f32[8,8,33,128]{3,1,2,0:T(8,128)} %multiply_subtract_fusion.2) | copy-start | bytes 3244036
  102.9 1.9 %copy-start.7 = (f32[8,9,32,128]{3,1,2,0:T(8,128)S(1)}, f32[8,9,32,128]{3,1,2,0:T(8,128)}, u32[]{:S(2)}) copy-start(f32[8,9,32,128]{3,1,2,0:T(8,128)} %multiply_subtract_fusion) | copy-start | bytes 3538948
  102.9 2.2 %copy-start.20 = (f32[8,8,32,128]{3,2,1,0:T(8,128)S(1)}, f32[8,8,32,128]{3,2,1,0:T(8,128)}, u32[]{:S(2)}) copy-start(f32[8,8,32,128]{3,2,1,0:T(8,128)} %param.4) | copy-start | bytes 3145732
where the time goes:
time: 112 us; the launch traced here: 111 us
  other arithmetic  43.6 us (39%)
  blocking collectives  30.1 us (27%)
  local copies, waits for them, and re-layouts  27.7 us (25%)
  starting transfers between devices  7.7 us (7%)
  between operations  1.96 us (2%)
    all_gather x1, blocking collectives, on_device(): lax.all_gather(inner_src, 'gy', axis=3, tiled=True)  15.1 us
    all_gather x1, blocking collectives, on_device(): lax.all_gather(outer_src, 'gy', axis=3, tiled=True)  15 us
    unnamed x50, other arithmetic  14.1 us
    unnamed x58, local copies, waits for them, and re-layouts  14 us
    ppermute x2, starting transfers between devices, with_halo(): after = lax.ppermute(first, axis, down)  7.32 us
    sub x3, other arithmetic, rusanov(): 0.5 * (flux_left + flux_right) - 0.5 * speed * (cons_right - cons_left)  5.88 us
    add x1, other arithmetic, section_update(): return 0.5 * old + 0.5 * (conserved(core) + time_step * rates)  4.85 us
    add x3, other arithmetic, sweep(): left = take(padded, 1, length - 2) + 0.5 * take(slope, 0, length - 3)  3.84 us
  transfers between devices with their start and end apart: 4, of which 0 were waited for; matrix products, arithmetic and copies ran while one was open for 37% of the time, Pallas kernels for 0%

commit v1 on v0

v1 whole, which is shorter than its diff:
```python
import functools

import jax
import jax.numpy as jnp
from jax import lax
from jax.experimental import pallas as pl
from jax.experimental.pallas import tpu as pltpu
from jax.sharding import PartitionSpec as P

gamma_gas = 5.0 / 3.0
omega_rate = 1.0
shear_rate = 1.5
time_step = 0.1

FIELDS = 8
EDGE = 4


def median0(a, b):
    return jnp.maximum(jnp.minimum(a, b), jnp.minimum(jnp.maximum(a, b), 0.0))


def half_slope(a, b):
    return 0.5 * median0(a, b)


def side(w, n):
    t, u = (n + 1) % 3, (n + 2) % 3
    rho, p = w[0], w[4]
    vn, vt, vu = w[1 + n], w[1 + t], w[1 + u]
    bn, bt, bu = w[5 + n], w[5 + t], w[5 + u]
    mn, mt, mu = rho * vn, rho * vt, rho * vu
    mnvn = mn * vn
    bn2 = bn * bn
    bt2 = bt * bt + bu * bu
    bsq = bn2 + bt2
    q = 0.5 * (mnvn + mt * vt + mu * vu) + p * (1.0 / (gamma_gas - 1.0))
    pm = 0.5 * bsq
    cons = [None] * FIELDS
    flux = [None] * FIELDS
    cons[0], cons[1 + n], cons[1 + t], cons[1 + u] = rho, mn, mt, mu
    cons[4] = q + pm
    cons[5 + n], cons[5 + t], cons[5 + u] = bn, bt, bu
    flux[0] = mn
    flux[1 + n] = mnvn + (p + pm - bn2)
    flux[1 + t] = mt * vn - bt * bn
    flux[1 + u] = mu * vn - bu * bn
    flux[4] = (q + p + bt2) * vn - bn * (vt * bt + vu * bu)
    flux[5 + t] = bt * vn - vt * bn
    flux[5 + u] = bu * vn - vu * bn
    a = gamma_gas * p
    diff = a - bsq
    disc = diff * diff + (4.0 * a) * bt2
    x = a + bsq + disc * lax.rsqrt(jnp.maximum(disc, 1e-30))
    speed = jnp.abs(vn) + x * lax.rsqrt((rho + rho) * x)
    return cons, flux, speed


def twice_face(left, right, n):
    cl, fl, sl = side(left, n)
    cr, fr, sr = side(right, n)
    s = jnp.maximum(sl, sr)
    out = []
    for j in range(FIELDS):
        jump = s * (cr[j] - cl[j])
        out.append(-jump if j == 5 + n else fl[j] + fr[j] - jump)
    return out


def rows_of(ref, x, nx):
    return [ref[f, pl.ds(x, 8, stride=nx), :] for f in range(FIELDS)]


def lanes():
    return lax.broadcasted_iota(jnp.int32, (8, 128), 1)


def pack_kernel(nx, par_ref, w_ref, xa_ref, xb_ref, ye_ref):
    odd = par_ref[0]
    first_a = (1 - odd) * (nx - 2)
    first_b = odd * (nx - 2)
    for f in range(FIELDS):
        for g in range(2):
            xa_ref[f, g] = w_ref[f, pl.ds(first_a + g, 8, stride=nx), :]
            xb_ref[f, g] = w_ref[f, pl.ds(first_b + g, 8, stride=nx), :]
    group = lanes() // EDGE
    for f in range(FIELDS):
        acc = jnp.zeros((8, 128), jnp.float32)
        for x in range(nx):
            row = w_ref[f, pl.ds(x, 8, stride=nx), :]
            acc = jnp.where(group == x, pltpu.roll(row, (EDGE * x + 2) % 128, 1), acc)
        ye_ref[f] = acc


def inner_kernel(nx, w_ref, old_ref, acc_ref, g_ref):
    def finish(x, div):
        w = rows_of(w_ref, x, nx)
        old = rows_of(old_ref, x, nx)
        rho, vx, vy, vz, p, bx, by, bz = w
        mx, my, mz = rho * vx, rho * vy, rho * vz
        energy = (
            p * (1.0 / (gamma_gas - 1.0))
            + 0.5 * (mx * vx + my * vy + mz * vz)
            + 0.5 * (bx * bx + by * by + bz * bz)
        )
        cons = [rho, mx, my, mz, energy, bx, by, bz]
        half_dt = 0.5 * time_step
        src = [None] * FIELDS
        src[1] = (half_dt * 2.0 * omega_rate) * my
        src[2] = (-half_dt * (2.0 - shear_rate) * omega_rate) * mx
        src[4] = (half_dt * shear_rate * omega_rate) * (mx * vy - bx * by)
        src[6] = (-half_dt * shear_rate * omega_rate) * bx
        for f in range(FIELDS):
            total = 0.5 * (old[f] + cons[f]) + (0.5 * half_dt) * div[f]
            acc_ref[f, x] = total if src[f] is None else total + src[f]

    def vertical(x):
        w = rows_of(w_ref, x, nx)
        left, right = [], []
        for f in range(FIELDS):
            up = pltpu.roll(w[f], 7, 0) - w[f]
            h = half_slope(pltpu.roll(up, 1, 0), up)
            left.append(w[f] + h)
            right.append(pltpu.roll(w[f] - h, 7, 0))
        g = twice_face(left, right, 2)
        return [pltpu.roll(v, 1, 0) - v for v in g]

    def radial(x):
        w0 = rows_of(w_ref, x - 1, nx)
        w1 = rows_of(w_ref, x, nx)
        w2 = rows_of(w_ref, x + 1, nx)
        w3 = rows_of(w_ref, x + 2, nx)
        left, right = [], []
        for f in range(FIELDS):
            mid = w2[f] - w1[f]
            left.append(w1[f] + half_slope(w1[f] - w0[f], mid))
            right.append(w2[f] - half_slope(mid, w3[f] - w2[f]))
        return twice_face(left, right, 0)

    finish(0, vertical(0))
    for f in range(FIELDS):
        g_ref[f] = jnp.zeros((8, 128), jnp.float32)

    def body(x, _):
        div = vertical(x)
        g = radial(x)
        for f in range(FIELDS):
            div[f] = div[f] + (g_ref[f] - g[f])
            g_ref[f] = g[f]
        finish(x, div)
        return 0

    lax.fori_loop(1, nx - 2, body, 0)
    div = vertical(nx - 2)
    finish(nx - 2, [div[f] + g_ref[f] for f in range(FIELDS)])
    finish(nx - 1, vertical(nx - 1))


def outer_kernel(
    nx, num_ref, frac_ref, w_ref, acc_ref, ye_ref, c_ref, y_ref, xa_ref, xb_ref, xe_ref,
    out_ref, h_ref, q_ref, x_ref, d_ref,
):
    odd_x, odd_y, shift, inner, outer = (num_ref[i] for i in range(5))
    frac = frac_ref[0]
    lane = lanes()
    scale = 0.25 * time_step

    ends = inner + outer
    frac = jnp.where(ends == 1, frac, 0.0)

    def window(b, e, s):
        amount = jnp.where(inner == 1, lax.rem(128 - s, 128), jnp.where(outer == 1, lax.rem(s, 128), 0))
        low = jnp.where(outer == 1, s, 0)
        high = jnp.where(inner == 1, 128 - s, 128)
        near = (lane >= low) & (lane < high)
        return jnp.where(near, pltpu.roll(b, amount, 1), pltpu.roll(e, amount, 1))

    for f in range(FIELDS):
        for g in range(2):
            b, e = xb_ref[f, g], xe_ref[f, g]
            ghost = (1.0 - frac) * window(b, e, shift) + frac * window(b, e, shift + 1)
            own = xa_ref[f, g]
            x_ref[f, g] = jnp.where(odd_x == 1, own, ghost)
            x_ref[f, 2 + g] = jnp.where(odd_x == 1, ghost, own)

    def radial(w0, w1, w2, w3):
        left, right = [], []
        for f in range(FIELDS):
            mid = w2[f] - w1[f]
            left.append(w1[f] + half_slope(w1[f] - w0[f], mid))
            right.append(w2[f] - half_slope(mid, w3[f] - w2[f]))
        return twice_face(left, right, 0)

    def ghosts(i):
        return [x_ref[f, i] for f in range(FIELDS)]

    def rows(x):
        return rows_of(w_ref, x, nx)

    for i, x in ((0, 0), (2, nx - 2)):
        if i == 0:
            strip = [ghosts(0), ghosts(1), rows(0), rows(1), rows(2)]
        else:
            strip = [rows(nx - 3), rows(nx - 2), rows(nx - 1), ghosts(2), ghosts(3)]
        g0 = radial(*strip[:4])
        g1 = radial(*strip[1:])
        for f in range(FIELDS):
            if i == 0:
                d_ref[f, 0] = g0[f] - g1[f]
                d_ref[f, 1] = g1[f]
            else:
                d_ref[f, 2] = -g0[f]
                d_ref[f, 3] = g0[f] - g1[f]

    place = lax.rem(lane, EDGE)
    from_left = place < 2
    left, right, outside = [], [], []
    for f in range(FIELDS):
        own = ye_ref[f]
        core, cross = c_ref[f], y_ref[f]
        near = jnp.where(odd_y == 1, core, cross)
        far = jnp.where(odd_y == 1, cross, core)
        h = jnp.where(from_left, near, far)
        h_ref[f] = h
        w0 = jnp.where(place == 1, pltpu.roll(h, 1, 1), pltpu.roll(own, 2, 1))
        w1 = jnp.where(place == 1, h, pltpu.roll(own, 1, 1))
        w2 = jnp.where(place == 1, pltpu.roll(own, 127, 1), h)
        w3 = jnp.where(place == 1, pltpu.roll(own, 126, 1), pltpu.roll(h, 127, 1))
        mid = w2 - w1
        left.append(w1 + half_slope(w1 - w0, mid))
        r = w2 - half_slope(mid, w3 - w2)
        right.append(r)
        outside.append(r)
    g = twice_face(left, right, 1)
    for f in range(FIELDS):
        q_ref[f] = g[f]

    def body(x, _):
        w = rows_of(w_ref, x, nx)
        turn = lax.rem(126 - EDGE * x + 512, 128)
        edge_turn = lax.rem(126 - EDGE * x + 512, 128)
        left, right = [], []
        for f in range(FIELDS):
            h = pltpu.roll(h_ref[f], turn, 1)
            up = pltpu.roll(jnp.where(lane == 0, h, w[f]), 127, 1) - w[f]
            down = w[f] - pltpu.roll(jnp.where(lane == 127, h, w[f]), 1, 1)
            s = half_slope(down, up)
            left.append(w[f] + s)
            right.append(pltpu.roll(w[f] - s, 127, 1))
        g = twice_face(left, right, 1)
        for f in range(FIELDS):
            q = pltpu.roll(q_ref[f], edge_turn, 1)
            lower = pltpu.roll(jnp.where(lane == 127, q, g[f]), 1, 1)
            upper = jnp.where(lane == 127, pltpu.roll(q, 127, 1), g[f])
            out_ref[f, pl.ds(x, 8, stride=nx), :] = acc_ref[f, x] + scale * (lower - upper)
        return 0

    lax.fori_loop(0, nx, body, 0)
    for i, x in ((0, 0), (1, 1), (2, nx - 2), (3, nx - 1)):
        for f in range(FIELDS):
            at = (f, pl.ds(x, 8, stride=nx), slice(None))
            out_ref[at] = out_ref[at] + scale * d_ref[f, i]


def swaps(nx, ny):
    def at(g, j):
        return (g % nx) * ny + j % ny

    grid = [(g, j) for g in range(nx) for j in range(ny)]
    core = [(at(g, j), at(g, j ^ 1)) for g, j in grid]
    cross = [(at(g, j), at(g, j + 1 if j % 2 else j - 1)) for g, j in grid]
    along = [(at(g, j), at(g ^ 1, j)) for g, j in grid]

    def ends(k):
        there = [(at(0, j), at(nx - 1, j + k)) for j in range(ny)]
        return there + [(b, a) for a, b in there]

    def other(k):
        inside = [(at(g, j), at(g + 1 if g % 2 else g - 1, j)) for g, j in grid if 0 < g < nx - 1]
        return inside + ends(k)

    return core, cross, along, other, ends


def on_device(old_state, section_prims, shear_whole, shear_frac):
    n_gx, n_gy = lax.axis_size("gx"), lax.axis_size("gy")
    gx, gy = lax.axis_index("gx"), lax.axis_index("gy")
    fields, nz, nx, cells = section_prims.shape
    assert (fields, nz, cells) == (FIELDS, 8, 128)
    assert EDGE * nx == cells and n_gx % 2 == 0 and n_gy % 2 == 0
    axes = ("gx", "gy")
    core, cross, along, other, ends = swaps(n_gx, n_gy)
    w = section_prims.reshape(fields, nz * nx, cells)
    old = old_state.reshape(fields, nz * nx, cells)
    f32 = jnp.float32
    vmem = pl.BlockSpec(memory_space=pltpu.VMEM)
    smem = pl.BlockSpec(memory_space=pltpu.SMEM)
    edge_rows = jax.ShapeDtypeStruct((fields, 2, nz, cells), f32)

    odd_x, odd_y = lax.rem(gx, 2), lax.rem(gy, 2)
    xa, xb, ye = pl.pallas_call(
        functools.partial(pack_kernel, nx),
        out_shape=(edge_rows, edge_rows, jax.ShapeDtypeStruct((fields, nz, cells), f32)),
        in_specs=[smem, vmem],
        out_specs=(vmem, vmem, vmem),
        name="pack",
    )(odd_x[None].astype(jnp.int32), w)

    c_in = lax.ppermute(ye, axes, core)
    y_in = lax.ppermute(ye, axes, cross)
    xa_in = lax.ppermute(xa, axes, along)

    def branch(k):
        def run(xb, w, old):
            xb_in = lax.ppermute(xb, axes, other(k))
            xe_in = lax.ppermute(xb, axes, ends(k + 1))
            acc = pl.pallas_call(
                functools.partial(inner_kernel, nx),
                out_shape=jax.ShapeDtypeStruct((fields, nx, nz, cells), f32),
                in_specs=[vmem, vmem],
                out_specs=vmem,
                scratch_shapes=[pltpu.VMEM((fields, nz, cells), f32)],
                cost_estimate=pl.CostEstimate(
                    flops=480 * nx * nz * cells, bytes_accessed=12 * fields * nx * nz * cells, transcendentals=0
                ),
                name="inner",
            )(w, old)
            return xb_in, xe_in, acc

        return run

    whole = lax.rem(shear_whole[0] // cells, n_gy)
    xb_in, xe_in, acc = lax.switch(whole, [branch(k) for k in range(n_gy)], xb, w, old)

    numbers = jnp.stack(
        [
            odd_x,
            odd_y,
            lax.rem(shear_whole[0], cells),
            (gx == 0).astype(jnp.int32),
            (gx == n_gx - 1).astype(jnp.int32),
        ]
    ).astype(jnp.int32)
    tile = (fields, nz, cells)
    out = pl.pallas_call(
        functools.partial(outer_kernel, nx),
        out_shape=jax.ShapeDtypeStruct((fields, nz * nx, cells), f32),
        in_specs=[smem, smem] + [vmem] * 8,
        out_specs=vmem,
        scratch_shapes=[
            pltpu.VMEM(tile, f32),
            pltpu.VMEM(tile, f32),
            pltpu.VMEM((fields, 4, nz, cells), f32),
            pltpu.VMEM((fields, 4, nz, cells), f32),
        ],
        name="outer",
    )(numbers, shear_frac, w, acc, ye, c_in, y_in, xa_in, xb_in, xe_in)
    return out.reshape(section_prims.shape)


def solution(mesh):
    in_specs = (P(None, None, "gx", "gy"), P(None, None, "gx", "gy"), P(), P())
    out_specs = P(None, None, "gx", "gy")
    return jax.shard_map(
        on_device, mesh=mesh, in_specs=in_specs, out_specs=out_specs, check_vma=False
    )
```

time: 112 us -> 38.1 us (0.34)
  other arithmetic: 43.6 us -> 0 us
  blocking collectives: 30.1 us -> 0 us
  local copies, waits for them, and re-layouts: 27.7 us -> 1.31 us
  Pallas kernels: 0 us -> 23.4 us
  starting transfers between devices: 7.7 us -> 11.8 us
    all_gather x2 -> x0, blocking collectives: 30.1 us -> none  [the longest x1 15.1 us: on_device(): lax.all_gather(inner_src, 'gy', axis=3, tiled=True)]
    pallas_call x0 -> x3, Pallas kernels: none -> 23.4 us  [the longest x1 13.6 us: on_device(): pl.pallas_call(functools.partial(outer_kernel, nx), out_shape=jax.ShapeDt...]
    unnamed x50 -> x0, other arithmetic: 14.1 us -> none
    unnamed x58 -> x8, local copies, waits for them, and re-layouts: 14 us -> 0.64 us
    add x4 -> x0, other arithmetic: 8.69 us -> none  [the longest x1 4.85 us: section_update(): return 0.5 * old + 0.5 * (conserved(core) + time_step * rates)]
    sub x6 -> x0, other arithmetic: 8.66 us -> none  [the longest x3 5.88 us: rusanov(): 0.5 * (flux_left + flux_right) - 0.5 * speed * (cons_right - cons_left)]
    mul x6 -> x0, other arithmetic: 6.25 us -> none  [the longest x3 3.37 us: minmod(): 0.5 * (jnp.sign(first) + jnp.sign(second))]
    slice x8 -> x0, local copies, waits for them, and re-layouts: 5.49 us -> none  [the longest x2 3.22 us: with_halo(): last = lax.slice_in_dim(shard, length - width, length, axis=dim)]
  transfers between devices with their start and end apart: 4 -> 5, of which waited for: 0 -> 0; matrix products, arithmetic and copies ran while one was open for 37% -> 2% of each run, Pallas kernels for 0% -> 19%
where the time goes in v1:
time: 38.1 us; the launch traced here: 38 us
  Pallas kernels  23.4 us (61%)
  starting transfers between devices  11.8 us (31%)
  between operations  1.38 us (4%)
  local copies, waits for them, and re-layouts  1.31 us (3%)
    pallas_call x1, Pallas kernels, on_device(): pl.pallas_call(functools.partial(outer_kernel, nx), out_shape=jax.ShapeDt...  13.6 us
    pallas_call x1, Pallas kernels, run(): pl.pallas_call(functools.partial(inner_kernel, nx), out_shape=jax.ShapeDt...  7.19 us
    ppermute x1, starting transfers between devices, run(): xe_in = lax.ppermute(xb, axes, ends(k + 1))  4 us
    ppermute x1, starting transfers between devices, on_device(): y_in = lax.ppermute(ye, axes, cross)  3.71 us
    ppermute x1, starting transfers between devices, on_device(): xa_in = lax.ppermute(xa, axes, along)  2.94 us
    pallas_call x1, Pallas kernels, on_device(): pl.pallas_call(functools.partial(pack_kernel, nx), out_shape=(edge_rows,...  2.6 us
    ppermute x1, starting transfers between devices, run(): xb_in = lax.ppermute(xb, axes, other(k))  1.17 us
  transfers between devices with their start and end apart: 5, of which 0 were waited for; matrix products, arithmetic and copies ran while one was open for 2% of the time, Pallas kernels for 19%

profile of v1, /device:TPU:0, one launch (start us, length us, event | category | flops | bytes accessed | tf_op | source)
XLA Modules:
  0.0 38.0 jit_solution(16056604805665654964)
XLA Ops:
  0.0 0.0 copy-start
  0.0 2.6 %pack.1 = (f32[8,2,8,128]{3,2,1,0:T(8,128)}, f32[8,2,8,128]{3,2,1,0:T(8,128)S(1)}, f32[8,8,128]{2,1,0:T(8,128)}) custom-call(s32[1]{0:T(128)} %bitcast.par_ref, f32[8,256,128]{2,1,0:T(8,128)} %bitcast.13), custom_call_target="tpu_custom_call" | custom-call | tf_op jit(solution)/shard_map/pack/pallas_call | solution.py:301
  2.6 2.9 %collective-permute-start.18 = (f32[8,2,8,128]{3,2,1,0:T(8,128)}, f32[8,2,8,128]{3,2,1,0:T(8,128)S(1)}, u32[]{:S(2)}, u32[]{:S(2)}) collective-permute-start(f32[8,2,8,128]{3,2,1,0:T(8,128)} %get-tuple-element.86), channel_id=1, source_target_pairs={{0,8},{1,9},{2,10},{3,11},{4,12},{5,13},{6,14},{7,15},{8,0},{9,1},... | collective-permute-start | bytes 196616 | tf_op jit(solution)/shard_map/ppermute | solution.py:311
  5.5 0.0 collective-permute-start.16
  5.5 3.7 %collective-permute-start.17 = (f32[8,8,128]{2,1,0:T(8,128)}, f32[8,8,128]{2,1,0:T(8,128)S(1)}, u32[]{:S(2)}, u32[]{:S(2)}) collective-permute-start(f32[8,8,128]{2,1,0:T(8,128)} %get-tuple-element.85.ye_ref), channel_id=1, source_target_pairs={{0,7},{1,2},{2,1},{3,4},{4,3},{5,6},{6,5},{7,0},{8,15},{9,10},{10,... | collective-permute-start | bytes 98312 | tf_op jit(solution)/shard_map/ppermute | solution.py:310
  10.6 0.0 copy-done
  10.6 12.4 %conditional.1 = (f32[8,2,8,128]{3,2,1,0:T(8,128)}, f32[8,2,8,128]{3,2,1,0:T(8,128)}, f32[8,32,8,128]{3,2,1,0:T(8,128)S(1)}) conditional(s32[]{:T(128)} %clamp.3, (f32[8,2,8,128]{3,2,1,0:T(8,128)S(1)}, f32[8,256,128]{2,1,0:T(8,128)S(1)}, f32[8,256,128]{2,1,0:T(8,128)}) %tuple.54, (f32[8,2,8,128]{3,2,1,0:T(8,128)S(1)}, ...), branch_computations={%region_0.1_spmd, %region_1.2_spmd, %region_2.3_spmd, %region_3.4_... | conditional | flops 15728640 | bytes 3670120 | solution.py:333
  10.6 1.2 %collective-permute-start.10 = (f32[8,2,8,128]{3,2,1,0:T(8,128)S(1)}, f32[8,2,8,128]{3,2,1,0:T(8,128)}, u32[]{:S(2)}, u32[]{:S(2)}) collective-permute-start(f32[8,2,8,128]{3,2,1,0:T(8,128)S(1)} %get-tuple-element.68), channel_id=1, source_target_pairs={{8,16},{9,17},{10,18},{11,19},{12,20},{13,21},{14,22},{15,23},{16,... | collective-permute-start | bytes 196616 | tf_op jit(solution)/shard_map/cond/branch_5_fun/ppermute | solution.py:315
  11.8 4.0 %collective-permute-start.11 = (f32[8,2,8,128]{3,2,1,0:T(8,128)S(1)}, f32[8,2,8,128]{3,2,1,0:T(8,128)}, u32[]{:S(2)}, u32[]{:S(2)}) collective-permute-start(f32[8,2,8,128]{3,2,1,0:T(8,128)S(1)} %get-tuple-element.68), channel_id=1, source_target_pairs={{0,30},{1,31},{2,24},{3,25},{4,26},{5,27},{6,28},{7,29},{30,0},{31... | collective-permute-start | bytes 196616 | tf_op jit(solution)/shard_map/cond/branch_5_fun/ppermute | solution.py:316
  15.8 7.2 %inner.13 = f32[8,32,8,128]{3,2,1,0:T(8,128)S(1)} custom-call(f32[8,256,128]{2,1,0:T(8,128)S(1)} %get-tuple-element.69.w_ref, f32[8,256,128]{2,1,0:T(8,128)} %get-tuple-element.70.old_ref), custom_call_target="tpu_custom_call" | custom-call | flops 15728640 | bytes 3145728 | tf_op jit(solution)/shard_map/cond/branch_5_fun/inner/pallas_call | solution.py:317
  23.0 0.0 collective-permute-done.10
  23.0 0.0 collective-permute-done.11
  23.0 0.7 %stack.31.num_ref = s32[5]{0:T(128)} concatenate(s32[1]{0:T(128)} %bitcast.par_ref, s32[1]{0:T(128)} %bitcast.1, s32[1]{0:T(128)} %bitcast.3, s32[1]{0:T(128)} %bitcast.4, s32[1]{0:T(128)} %bitcast.5), dimensions={0} | concatenate | bytes 40 | tf_op jit(solution)/shard_map/stack | solution.py:335
  23.7 0.0 collective-permute-done.16.c_ref
  23.7 0.0 copy-start.2
  23.7 0.0 collective-permute-done.17.y_ref
  23.7 0.0 copy-start.3
  23.7 0.0 collective-permute-done.18.xa_ref
  23.7 0.0 copy-start.1
  23.7 0.6 %copy-done.2 = f32[8,8,128]{2,1,0:T(8,128)} copy-done((f32[8,8,128]{2,1,0:T(8,128)}, f32[8,8,128]{2,1,0:T(8,128)S(1)}, u32[]{:S(2)}) %copy-start.2) | copy-done | bytes 32792
  24.3 0.0 copy-done.3
  24.3 0.1 copy-done.1
  24.4 13.6 %outer.1 = f32[8,256,128]{2,1,0:T(8,128)} custom-call(s32[5]{0:T(128)} %stack.31.num_ref, f32[1]{0:T(128)S(6)} %copy.30.frac_ref, f32[8,256,128]{2,1,0:T(8,128)S(1)} %bitcast.22, f32[8,32,8,128]{3,2,1,0:T(8,128)S(1)} %get-tuple-element.84.acc_ref, f32[8,8,128]{2,1,0:T(8,128)} %get-tuple-element.85.ye_ref, f32[8,8,128]{2,1,0:T(8,128)} %copy-done.2, ...), custom_call_target="tpu_custom_call" | custom-call | tf_op jit(solution)/shard_map/outer/pallas_call | solution.py:345
Async XLA Ops:
  0.0 10.6 %copy-start = (f32[8,8,32,128]{3,2,1,0:T(8,128)S(1)}, f32[8,8,32,128]{3,2,1,0:T(8,128)}, u32[]{:S(2)}) copy-start(f32[8,8,32,128]{3,2,1,0:T(8,128)} %param.13) | copy-start | bytes 3145732
  2.6 21.1 %collective-permute-start.18 = (f32[8,2,8,128]{3,2,1,0:T(8,128)}, f32[8,2,8,128]{3,2,1,0:T(8,128)S(1)}, u32[]{:S(2)}, u32[]{:S(2)}) collective-permute-start(f32[8,2,8,128]{3,2,1,0:T(8,128)} %get-tuple-element.86), channel_id=1, source_target_pairs={{0,8},{1,9},{2,10},{3,11},{4,12},{5,13},{6,14},{7,15},{8,0},{9,1},... | collective-permute-start | bytes 196616 | tf_op jit(solution)/shard_map/ppermute | solution.py:311
  5.5 18.2 %collective-permute-start.16 = (f32[8,8,128]{2,1,0:T(8,128)}, f32[8,8,128]{2,1,0:T(8,128)S(1)}, u32[]{:S(2)}, u32[]{:S(2)}) collective-permute-start(f32[8,8,128]{2,1,0:T(8,128)} %get-tuple-element.85.ye_ref), channel_id=1, source_target_pairs={{0,1},{1,0},{2,3},{3,2},{4,5},{5,4},{6,7},{7,6},{8,9},{9,8},{10,11... | collective-permute-start | bytes 98312 | tf_op jit(solution)/shard_map/ppermute | solution.py:309
  5.5 18.2 %collective-permute-start.17 = (f32[8,8,128]{2,1,0:T(8,128)}, f32[8,8,128]{2,1,0:T(8,128)S(1)}, u32[]{:S(2)}, u32[]{:S(2)}) collective-permute-start(f32[8,8,128]{2,1,0:T(8,128)} %get-tuple-element.85.ye_ref), channel_id=1, source_target_pairs={{0,7},{1,2},{2,1},{3,4},{4,3},{5,6},{6,5},{7,0},{8,15},{9,10},{10,... | collective-permute-start | bytes 98312 | tf_op jit(solution)/shard_map/ppermute | solution.py:310
  10.6 12.4 %collective-permute-start.10 = (f32[8,2,8,128]{3,2,1,0:T(8,128)S(1)}, f32[8,2,8,128]{3,2,1,0:T(8,128)}, u32[]{:S(2)}, u32[]{:S(2)}) collective-permute-start(f32[8,2,8,128]{3,2,1,0:T(8,128)S(1)} %get-tuple-element.68), channel_id=1, source_target_pairs={{8,16},{9,17},{10,18},{11,19},{12,20},{13,21},{14,22},{15,23},{16,... | collective-permute-start | bytes 196616 | tf_op jit(solution)/shard_map/cond/branch_5_fun/ppermute | solution.py:315
  11.8 11.2 %collective-permute-start.11 = (f32[8,2,8,128]{3,2,1,0:T(8,128)S(1)}, f32[8,2,8,128]{3,2,1,0:T(8,128)}, u32[]{:S(2)}, u32[]{:S(2)}) collective-permute-start(f32[8,2,8,128]{3,2,1,0:T(8,128)S(1)} %get-tuple-element.68), channel_id=1, source_target_pairs={{0,30},{1,31},{2,24},{3,25},{4,26},{5,27},{6,28},{7,29},{30,0},{31... | collective-permute-start | bytes 196616 | tf_op jit(solution)/shard_map/cond/branch_5_fun/ppermute | solution.py:316
  23.7 0.6 %copy-start.2 = (f32[8,8,128]{2,1,0:T(8,128)}, f32[8,8,128]{2,1,0:T(8,128)S(1)}, u32[]{:S(2)}) copy-start(f32[8,8,128]{2,1,0:T(8,128)S(1)} %collective-permute-done.16.c_ref) | copy-start | bytes 98308
  23.7 0.6 %copy-start.3 = (f32[8,8,128]{2,1,0:T(8,128)}, f32[8,8,128]{2,1,0:T(8,128)S(1)}, u32[]{:S(2)}) copy-start(f32[8,8,128]{2,1,0:T(8,128)S(1)} %collective-permute-done.17.y_ref) | copy-start | bytes 98308
  23.7 0.6 %copy-start.1 = (f32[8,2,8,128]{3,2,1,0:T(8,128)}, f32[8,2,8,128]{3,2,1,0:T(8,128)S(1)}, u32[]{:S(2)}) copy-start(f32[8,2,8,128]{3,2,1,0:T(8,128)S(1)} %collective-permute-done.18.xa_ref) | copy-start | bytes 196612
